TPU v7x, 256 devices: a whole 4x4x8 slice. The times are simulated.
256 devices in a mesh: view: 64 (over z, y, core), feat: 4 (over x).
Axes of the slice: x: 4, y: 4, z: 8, core: 2. Of those that a mesh axis runs over, the one named last changes fastest.
Arguments:
- points: bfloat16 [4096, 768, 128], P('view', 'feat'), may hold values from -6 to 6
- head_weight: bfloat16 [768, 768], P('feat'), may hold values from -0.21875 to 0.21875
- teacher: bfloat16 [768, 128, 1369], P('feat', 'view'), may hold values from -6 to 6
- splat_weight: bfloat16 [128, 64, 74, 128], P('view'), may hold values from 0 to 0.19921875
- block_owner: int32 [128, 16, 4], P('view'), may hold values from 0 to 63, all different within a row; in each aligned block of 32 rows (0 to 31, 32 to 63, ..., all dimensions but the last counted through in order) at most 3 rows name the same one
- block_local: int32 [128, 64], P('view'), may hold values from 0 to 63
- block_row: int32 [128, 64], P('view'), may hold values from 0 to 35, as said below
Outputs:
- grad_points: bfloat16 [4096, 768, 128], P('view', 'feat')
- head_grad: float32 [768, 768], P('feat')
Inputs may be any that keep to these rules, and one draw needn't show every extreme that they name: `block_owner`: over the 128 list entries of the views of one index of view, no owner appears more than 3 times, and some owner appears exactly 3 times. `block_row`: each view's list holds every value from 0 to 35 at least once.
All inputs are finite; a program needn't handle non-finite values.
Results may differ from a plain program's by a relative error of at most 0.0064.
Values may be sent and summed in bfloat16 or wider, within the bound.
A program may use at most 128 MiB of HBM per device.

v0:
```python
import jax
import jax.numpy as jnp
from jax import lax
from jax.sharding import PartitionSpec as P

GRID = 37
BAND = 2
BLOCK = 128


def slot_plan(owners, peer_count, capacity):
    total_requests = owners.shape[0]
    positions = jnp.arange(total_requests, dtype=jnp.int32)
    earlier = (owners[:, None] == owners[None, :]) & (positions[None, :] < positions[:, None])
    slot_rank = jnp.sum(earlier.astype(jnp.int32), axis=1)
    target = owners * capacity + slot_rank
    slot_ids = jnp.arange(peer_count * capacity, dtype=jnp.int32)
    matches = target[None, :] == slot_ids[:, None]
    source = jnp.sum(jnp.where(matches, positions[None, :], 0), axis=1)
    filled = jnp.any(matches, axis=1)
    return (target, source, filled)


def per_device(points, head_weight, teacher, splat_weight, block_owner, block_local, block_row):
    peer_count = lax.axis_size("view")
    local_width = points.shape[1]
    view_count = splat_weight.shape[0]
    visible = splat_weight.shape[1]
    requests = view_count * visible
    capacity = max(3, (3 * requests + 2 * peer_count - 1) // (2 * peer_count))
    owners = block_owner.reshape(requests)
    local_ids = block_local.reshape(requests)
    target, source, filled = slot_plan(owners, peer_count, capacity)
    wanted = jnp.where(filled, jnp.take(local_ids, source), 0)
    columns = jnp.arange(GRID, dtype=jnp.int32)
    row_masks = [
        (block_row[:, :, None] + offset == columns[None, None, :]).astype(jnp.bfloat16)
        for offset in range(BAND)
    ]
    empty_bf = jnp.zeros((), jnp.bfloat16)
    asked_ids = lax.all_to_all(wanted, "view", split_axis=0, concat_axis=0, tiled=True)
    sent_rows = jnp.take(points, asked_ids, axis=0)
    arrived = lax.all_to_all(sent_rows, "view", split_axis=0, concat_axis=0, tiled=True)
    fetched = jnp.take(arrived, target, axis=0).reshape(view_count, visible, local_width, BLOCK)
    contrib = jnp.einsum(
        "vjcp,vjdp->vjcd", splat_weight, fetched, preferred_element_type=jnp.float32
    ).astype(jnp.bfloat16)
    rendered = jnp.zeros((view_count, GRID, GRID, local_width), jnp.float32)
    for offset in range(BAND):
        band_part = contrib[:, :, offset * GRID : (offset + 1) * GRID, :]
        rendered = rendered + jnp.einsum(
            "vjr,vjcd->vrcd", row_masks[offset], band_part, preferred_element_type=jnp.float32
        )
    rendered_rows = rendered.astype(jnp.bfloat16).reshape(view_count * GRID * GRID, local_width)
    pixel_rows = rendered_rows.shape[0]
    teacher_width = head_weight.shape[1]
    local_teacher = teacher.shape[0]
    contract_first = (((0,), (1,)), ((), ()))
    projected = lax.psum_scatter(
        lax.dot_general(
            head_weight, rendered_rows, contract_first, preferred_element_type=jnp.float32
        ),
        "feat",
        scatter_dimension=0,
        tiled=True,
    )
    square_sum = lax.psum(jnp.sum(projected * projected, axis=0), "feat")
    scale_rows = jnp.sqrt(square_sum / teacher_width + 1e-06)
    normed = projected / scale_rows[None, :]
    target_feat = teacher.reshape(local_teacher, pixel_rows).astype(jnp.float32)
    residual = normed - target_feat
    row_dot = lax.psum(jnp.sum(residual * normed, axis=0), "feat")
    grad_proj = (
        (residual - normed * (row_dot / teacher_width)[None, :]) / scale_rows[None, :]
    ).astype(jnp.bfloat16)
    shard_part = lax.all_gather(grad_proj, "feat", axis=0, tiled=True)
    grad_image = lax.dot_general(
        shard_part, head_weight, contract_first, preferred_element_type=jnp.float32
    )
    column_part = lax.dot_general(
        rendered_rows, shard_part, contract_first, preferred_element_type=jnp.float32
    )
    grad_head = column_part
    grad_image, grad_head = (grad_image, grad_head)
    head_grad = lax.psum(grad_head, "view") / (view_count * peer_count * GRID)
    grad_image = grad_image.astype(jnp.bfloat16).reshape(view_count, GRID, GRID, local_width)
    pieces = [
        jnp.einsum("vjr,vrcd->vjcd", row_mask, grad_image, preferred_element_type=jnp.float32)
        for row_mask in row_masks
    ]
    grad_contrib = jnp.concatenate(pieces, axis=2).astype(jnp.bfloat16)
    grad_block = jnp.einsum(
        "vjcp,vjcd->vjdp", splat_weight, grad_contrib, preferred_element_type=jnp.float32
    ).astype(jnp.bfloat16)
    grad_block = grad_block.reshape(requests, local_width, BLOCK)
    packed = jnp.where(filled[:, None, None], jnp.take(grad_block, source, axis=0), empty_bf)
    landed = lax.all_to_all(packed, "view", split_axis=0, concat_axis=0, tiled=True)
    summed = jax.ops.segment_sum(
        landed.astype(jnp.float32), asked_ids, num_segments=points.shape[0]
    )
    grad_points = summed.astype(jnp.bfloat16)
    return (grad_points, head_grad)


def solution(mesh):
    placed = (
        P("view", "feat", None),
        P("feat", None),
        P("feat", "view", None),
        P("view", None, None, None),
        P("view", None, None),
        P("view", None),
        P("view", None),
    )
    return jax.shard_map(
        per_device,
        mesh=mesh,
        in_specs=placed,
        out_specs=(P("view", "feat", None), P("feat", None)),
        check_vma=False,
    )
```

profile of v0, /device:TPU:1, one launch (start us, length us, event | category | flops | bytes accessed | tf_op | source)
XLA Modules:
  0.0 846.6 jit_solution(4426664382847408768)
XLA Ops:
  7.2 0.9 copy.41
  8.6 0.8 reshape.193
  9.7 1.6 gather_fusion
  11.4 22.4 %all_to_all.19 = s32[64,3,1]{1,2,0:T(1,128)S(1)} all-to-all(s32[64,3,1]{1,2,0:T(1,128)S(1)} %bitcast.40), channel_id=1, replica_groups=mesh['view'=64,'feat'=4] {'view'}, dimensions={0} | all-to-all | bytes 1536 | tf_op jit(solution)/shard_map/all_to_all | solution.py:41
  34.0 0.5 broadcast.172
  34.5 0.7 reduce.5
  35.4 9.7 %gather_fusion.1 = bf16[192,192,128]{2,1,0:T(8,128)(2,1)} fusion(bf16[64,192,128]{2,1,0:T(8,128)(2,1)S(1)} %copy-done, s32[1024]{0:T(1024)S(1)} %pad_clamp_fusion.1), kind=kCustom, calls=%fused_computation.1 | custom fusion | bytes 18875136 | tf_op jit(solution)/shard_map/jit(_take)/gather | solution.py:42
  45.1 8.2 broadcast_select_fusion
  53.3 5.9 all-to-all-start.1
  59.2 0.5 reduce-scatter.4.cloned.1.call-start
  60.2 204.1 %all-to-all-done.1 = bf16[192,192,128]{2,1,0:T(8,128)(2,1)} async-done(((bf16[192,192,128]{2,1,0:T(8,128)(2,1)}), bf16[192,192,128]{2,1,0:T(8,128)(2,1)}, u32[]{:S(2)}, u32[]{:S(2)}) %all-to-all-start.1) | async-done | bytes 9437216 | tf_op jit(solution)/shard_map/all_to_all | solution.py:43
  264.3 7.7 gather_fusion.2
  272.0 9.3 %convert_bitcast_fusion = bf16[2,64,74,192]{3,2,1,0:T(8,128)(2,1)} fusion(bf16[2,64,192,128]{3,2,1,0:T(8,128)(2,1)} %bitcast.38, pred[2,64]{1,0:T(4,128)(4,1)S(1)} %compare_and_fusion.1, bf16[2,64,74,128]{3,1,2,0:T(8,128)(2,1)S(1)} %copy-done.5), kind=kOutput, calls=%fused_computation.13 | convolution fusion | flops 470532096 | bytes 12353664 | tf_op jit(solution)/shard_map/vjcp,vjdp->vjcd/dot_general | solution.py:45
  281.3 4.3 fusion.36
  285.6 0.6 fusion.11
  286.2 0.7 add_convert_fusion
  286.9 0.3 copy.48
  287.2 0.7 reshape.194
  287.9 4.5 convolution_bitcast_fusion
  292.5 9.0 %copy.57 = f32[768,2738]{1,0:T(8,128)} copy(f32[768,2738]{0,1:T(8,128)} %convolution_bitcast_fusion) | data formatting | bytes 16822272
  301.6 1.2 copy-done.7
  302.8 1.7 reshape.197
  304.4 83.7 %reduce-scatter.4.cloned.1.call-done = f32[192,2738]{1,0:T(8,128)} async-done(((f32[768,2738]{1,0:T(8,128)}), f32[192,2738]{1,0:T(8,128)}) %reduce-scatter.4.cloned.1.call-update) | async-done | bytes 2102800 | tf_op jit(solution)/shard_map/reduce_scatter | solution.py:59
  388.2 3.4 copy.58
  391.6 2.2 multiply_reduce_fusion
  393.8 11.2 %psum.21 = f32[2738]{0:T(1024)S(1)} all-reduce(f32[2738]{0:T(1024)S(1)} %multiply_reduce_fusion), channel_id=1, replica_groups=mesh['view'=64,'feat'=4] {'feat'}, use_global_device_ids=true, to_apply=%region_5.6 | all-reduce | flops 2738 | bytes 21904 | tf_op jit(solution)/shard_map/psum | solution.py:67
  405.0 1.9 multiply_reduce_fusion.1
  406.9 11.3 %psum.22 = f32[2738]{0:T(1024)S(1)} all-reduce(f32[2738]{0:T(1024)S(1)} %multiply_reduce_fusion.1), channel_id=1, replica_groups=mesh['view'=64,'feat'=4] {'feat'}, use_global_device_ids=true, to_apply=%region_7.8 | all-reduce | flops 2738 | bytes 21904 | tf_op jit(solution)/shard_map/psum | solution.py:72
  418.3 3.0 divide_convert_fusion
  421.3 58.4 %all-gather.2.cloned.1.call-done = bf16[768,2738]{1,0:T(8,128)(2,1)} async-done(((bf16[192,2738]{1,0:T(8,128)(2,1)}), bf16[768,2738]{1,0:T(8,128)(2,1)}) %all-gather.2.cloned.1.call-update) | async-done | bytes 4205584 | tf_op jit(solution)/shard_map/all_gather | solution.py:76
  479.7 3.2 convolution_convert_fusion
  483.0 1.2 copy.50
  484.2 0.7 reshape.195
  484.9 0.8 convolution_convert_fusion.1
  485.8 0.8 convolution_convert_fusion.2
  486.6 0.8 pad_maximum_fusion
  487.4 0.9 copy-done.6
  488.3 7.4 fusion.5
  495.7 12.4 %gather_fusion.3 = bf16[192,192,128]{2,1,0:T(8,128)(2,1)} fusion(bf16[128,192,128]{2,1,0:T(8,128)(2,1)} %bitcast.37, s32[1024]{0:T(1024)S(1)} %pad_clamp_fusion.2), kind=kCustom, calls=%fused_computation.3 | custom fusion | bytes 18875136 | tf_op jit(solution)/shard_map/jit(_take)/gather | solution.py:96
  508.2 9.9 %select_select_fusion = bf16[192,192,128]{2,1,0:T(8,128)(2,1)} fusion(bf16[192,192,128]{2,1,0:T(8,128)(2,1)} %gather_fusion.3, pred[192]{0:T(512)(128)(4,1)S(1)} %compare_and_fusion.2, pred[192]{0:T(512)(128)(4,1)S(1)} %fusion.21), kind=kLoop, calls=%fused_computation.5 | loop fusion | flops 9437184 | bytes 18874752 | tf_op jit(solution)/shard_map/jit(_where)/select_n | solution.py:96
  518.1 11.2 %all-to-all-start.2 = ((bf16[192,192,128]{2,1,0:T(8,128)(2,1)}), bf16[192,192,128]{2,1,0:T(8,128)(2,1)}, u32[]{:S(2)}, u32[]{:S(2)}) async-start(bf16[192,192,128]{2,1,0:T(8,128)(2,1)} %select_select_fusion), calls=%async_computation.2 | async-start | bytes 18874368 | tf_op jit(solution)/shard_map/all_to_all | solution.py:97
  529.3 4.6 fusion.37
  533.9 235.7 %all-reduce.2.cloned.1.call-done = f32[192,768]{1,0:T(8,128)} async-done(((f32[192,768]{1,0:T(8,128)}), f32[192,768]{1,0:T(8,128)}) %all-reduce.2.cloned.1.call-update) | async-done | bytes 589840 | tf_op jit(solution)/shard_map/psum | solution.py:85
  769.6 1.9 broadcast_multiply_fusion
  771.5 12.4 %convert_element_type.45 = f32[192,192,128]{2,1,0:T(8,128)} convert(bf16[192,192,128]{2,1,0:T(8,128)(2,1)} %all-to-all-done.2) | non-fusion elementwise | flops 4718592 | bytes 28311552 | tf_op jit(solution)/shard_map/convert_element_type | solution.py:99
  783.9 3.4 broadcast_in_dim.79
  787.3 47.5 %scatter_fusion = f32[64,192,128]{2,1,0:T(8,128)} fusion(f32[64,192,128]{2,1,0:T(8,128)} %broadcast_in_dim.79, s32[192]{0:T(256)S(1)} %reshape.232, f32[192,192,128]{2,1,0:T(8,128)} %convert_element_type.45), kind=kCustom, calls=%fused_computation.4 | custom fusion | flops 4718592 | bytes 56623872 | tf_op jit(solution)/shard_map/scatter-add | solution.py:98
  834.8 5.0 convert_element_type.46
  (54 shorter events, 1.9 us)
Async XLA Ops:
  7.2 28.2 %copy-start = (bf16[64,192,128]{2,1,0:T(8,128)(2,1)S(1)}, bf16[64,192,128]{2,1,0:T(8,128)(2,1)}, u32[]{:S(2)}) copy-start(bf16[64,192,128]{2,1,0:T(8,128)(2,1)} %param.7) | copy-start | bytes 9437188
  53.3 6.4 copy-start.9
  53.3 6.9 copy-start.10
  53.3 211.0 %all-to-all-start.1 = ((bf16[192,192,128]{2,1,0:T(8,128)(2,1)}), bf16[192,192,128]{2,1,0:T(8,128)(2,1)}, u32[]{:S(2)}, u32[]{:S(2)}) async-start(bf16[192,192,128]{2,1,0:T(8,128)(2,1)} %broadcast_select_fusion), calls=%async_computation.1 | async-start | bytes 18874368 | tf_op jit(solution)/shard_map/all_to_all | solution.py:43
  59.2 328.9 %reduce-scatter.4.cloned.1.call-start = ((), (), s32[]{:S(2)}) async-start(), calls=%async_computation.6 | async-start | bytes 10813440 | tf_op jit(solution)/shard_map/reduce_scatter | solution.py:59
  60.2 211.8 %copy-start.5 = (bf16[2,64,74,128]{3,1,2,0:T(8,128)(2,1)S(1)}, bf16[2,64,74,128]{3,1,2,0:T(8,128)(2,1)}, u32[]{:S(2)}) copy-start(bf16[2,64,74,128]{3,1,2,0:T(8,128)(2,1)} %param.10) | copy-start | bytes 7274500
  286.9 1.0 copy-start.8
  287.9 4.5 copy-start.3
  301.5 1.2 copy-start.7
  301.5 178.2 %all-gather.2.cloned.1.call-start = ((), (), s32[]{:S(2)}) async-start(), calls=%async_computation.4 | async-start | bytes 5406720 | tf_op jit(solution)/shard_map/all_gather | solution.py:76
  388.2 16.8 %copy-start.2 = (f32[192,2738]{1,0:T(8,128)S(1)}, f32[192,2738]{1,0:T(8,128)}, u32[]{:S(2)}) copy-start(f32[192,2738]{1,0:T(8,128)} %reduce-scatter.4.cloned.1.call-done) | copy-start | bytes 6308356
  486.6 1.7 copy-start.6
  518.0 11.2 %copy-start.4 = (bf16[2738,192]{1,0:T(8,128)(2,1)S(1)}, bf16[2738,192]{1,0:T(8,128)(2,1)}, u32[]{:S(2)}) copy-start(bf16[2738,192]{1,0:T(8,128)(2,1)} %copy-done.3) | copy-start | bytes 3154180
  518.1 253.5 %all-to-all-start.2 = ((bf16[192,192,128]{2,1,0:T(8,128)(2,1)}), bf16[192,192,128]{2,1,0:T(8,128)(2,1)}, u32[]{:S(2)}, u32[]{:S(2)}) async-start(bf16[192,192,128]{2,1,0:T(8,128)(2,1)} %select_select_fusion), calls=%async_computation.2 | async-start | bytes 18874368 | tf_op jit(solution)/shard_map/all_to_all | solution.py:97
  529.2 240.4 %all-reduce.2.cloned.1.call-start = ((), (), s32[]{:S(2)}) async-start(), calls=%async_computation.5 | async-start | bytes 1179648 | tf_op jit(solution)/shard_map/psum | solution.py:85
  787.3 52.5 %copy-start.1 = (bf16[64,192,128]{2,1,0:T(8,128)(2,1)S(1)}, bf16[64,192,128]{2,1,0:T(8,128)(2,1)}, u32[]{:S(2)}) copy-start(bf16[64,192,128]{2,1,0:T(8,128)(2,1)} %param.7) | copy-start | bytes 9437188
Sparse Core Ops, SparseCore 0:
  301.7 86.4 reduce-scatter.3
  421.4 58.2 all-gather.1
  534.1 235.4 all-reduce.1
where the time goes:
time: 853 us; the launch traced here: 847 us
  waiting for transfers between devices  582 us (68%)
  other arithmetic  94.1 us (11%)
  local copies, waits for them, and re-layouts  61.6 us (7%)
  blocking collectives  44.9 us (5%)
  matrix products  32.1 us (4%)
  starting transfers between devices  17.7 us (2%)
  between operations  14.3 us (2%)
    psum x1, waiting for transfers between devices, per_device(): head_grad = lax.psum(grad_head, 'view') / (view_count * peer_count * GRID)  236 us
    all_to_all x1, waiting for transfers between devices, per_device(): lax.all_to_all(sent_rows, 'view', split_axis=0, concat_axis=0, tiled=True)  204 us
    reduce_scatter x1, waiting for transfers between devices, per_device(): lax.psum_scatter(lax.dot_general(head_weight, rendered_rows, contract_fir...  83.7 us
    all_gather x1, waiting for transfers between devices, per_device(): shard_part = lax.all_gather(grad_proj, 'feat', axis=0, tiled=True)  58.4 us
    scatter-add x1, other arithmetic, per_device(): jax.ops.segment_sum(landed.astype(jnp.float32), asked_ids, num_segments=p...  47.5 us
    all_to_all x1, blocking collectives, per_device(): lax.all_to_all(wanted, 'view', split_axis=0, concat_axis=0, tiled=True)  22.4 us
  transfers between devices with their start and end apart: 5, of which 4 were waited for; matrix products, arithmetic and copies ran while one was open for 1% of the time, Pallas kernels for 0%

commit v1 on v0

--- a/solution.py
+++ b/solution.py
@@ -6,6 +6,12 @@
 GRID = 37
 BAND = 2
 BLOCK = 128
+
+
+def summed_here(x, axis):
+    terms = lax.all_gather(x, axis, axis=0, tiled=False)
+    result = terms.sum(axis=0)
+    return result
 
 
 def slot_plan(owners, peer_count, capacity):
@@ -82,7 +88,7 @@
     )
     grad_head = column_part
     grad_image, grad_head = (grad_image, grad_head)
-    head_grad = lax.psum(grad_head, "view") / (view_count * peer_count * GRID)
+    head_grad = summed_here(grad_head, "view") / (view_count * peer_count * GRID)
     grad_image = grad_image.astype(jnp.bfloat16).reshape(view_count, GRID, GRID, local_width)
     pieces = [
         jnp.einsum("vjr,vrcd->vjcd", row_mask, grad_image, preferred_element_type=jnp.float32)

time: 853 us -> 934 us (1.095)
  blocking collectives: 44.9 us -> 361 us
  waiting for transfers between devices: 582 us -> 346 us
  starting transfers between devices: 17.7 us -> 6.42 us
  other arithmetic: 94.1 us -> 104 us
    all_to_all x0 -> x1, blocking collectives: none -> 307 us  [per_device(): lax.all_to_all(packed, 'view', split_axis=0, concat_axis=0, tiled=True)]
    psum x1 -> x0, waiting for transfers between devices: 236 us -> none  [per_device(): head_grad = lax.psum(grad_head, 'view') / (view_count * peer_count * GRID)]
    reduce_sum x0 -> x1, other arithmetic: none -> 14.5 us  [summed_here(): result = terms.sum(axis=0)]
    all_to_all x1 -> x0, starting transfers between devices: 11.2 us -> none  [per_device(): lax.all_to_all(packed, 'view', split_axis=0, concat_axis=0, tiled=True)]
  transfers between devices with their start and end apart: 5 -> 4, of which waited for: 4 -> 3; matrix products, arithmetic and copies ran while one was open for 1% -> 11% of each run, Pallas kernels for 0% -> 0%
where the time goes in v1:
time: 934 us; the launch traced here: 926 us
  blocking collectives  361 us (39%)
  waiting for transfers between devices  346 us (37%)
  other arithmetic  104 us (11%)
  local copies, waits for them, and re-layouts  61.7 us (7%)
  matrix products  32.4 us (3%)
  between operations  14.3 us (2%)
    all_to_all x1, blocking collectives, per_device(): lax.all_to_all(packed, 'view', split_axis=0, concat_axis=0, tiled=True)  307 us
    all_to_all x1, waiting for transfers between devices, per_device(): lax.all_to_all(sent_rows, 'view', split_axis=0, concat_axis=0, tiled=True)  204 us
    reduce_scatter x1, waiting for transfers between devices, per_device(): lax.psum_scatter(lax.dot_general(head_weight, rendered_rows, contract_fir...  83.7 us
    all_gather x1, waiting for transfers between devices, per_device(): shard_part = lax.all_gather(grad_proj, 'feat', axis=0, tiled=True)  58.4 us
    scatter-add x1, other arithmetic, per_device(): jax.ops.segment_sum(landed.astype(jnp.float32), asked_ids, num_segments=p...  47.1 us
    all_to_all x1, blocking collectives, per_device(): lax.all_to_all(wanted, 'view', split_axis=0, concat_axis=0, tiled=True)  22.4 us
    psum x1, blocking collectives, per_device(): row_dot = lax.psum(jnp.sum(residual * normed, axis=0), 'feat')  20.1 us
  transfers between devices with their start and end apart: 4, of which 3 were waited for; matrix products, arithmetic and copies ran while one was open for 11% of the time, Pallas kernels for 0%

profile of v1, /device:TPU:1, one launch (start us, length us, event | category | flops | bytes accessed | tf_op | source)
XLA Modules:
  0.0 926.3 jit_solution(1917710731818246718)
XLA Ops:
  7.2 0.9 copy.41
  8.8 0.8 reshape.193
  9.6 1.5 gather_fusion
  11.4 22.4 %all_to_all.19 = s32[64,3,1]{1,2,0:T(1,128)S(1)} all-to-all(s32[64,3,1]{1,2,0:T(1,128)S(1)} %bitcast.42), channel_id=1, replica_groups=mesh['view'=64,'feat'=4] {'view'}, dimensions={0} | all-to-all | bytes 1536 | tf_op jit(solution)/shard_map/all_to_all | solution.py:47
  33.8 0.5 broadcast.172
  34.3 0.7 reduce.5
  35.4 9.7 %gather_fusion.1 = bf16[192,192,128]{2,1,0:T(8,128)(2,1)} fusion(bf16[64,192,128]{2,1,0:T(8,128)(2,1)S(1)} %copy-done, s32[1024]{0:T(1024)S(1)} %pad_clamp_fusion.1), kind=kCustom, calls=%fused_computation.1 | custom fusion | bytes 18875136 | tf_op jit(solution)/shard_map/jit(_take)/gather | solution.py:48
  45.1 8.3 broadcast_select_fusion
  53.3 5.9 all-to-all-start.1
  59.3 0.4 reduce-scatter.4.cloned.1.call-start
  60.1 204.2 %all-to-all-done.1 = bf16[192,192,128]{2,1,0:T(8,128)(2,1)} async-done(((bf16[192,192,128]{2,1,0:T(8,128)(2,1)}), bf16[192,192,128]{2,1,0:T(8,128)(2,1)}, u32[]{:S(2)}, u32[]{:S(2)}) %all-to-all-start.1) | async-done | bytes 9437216 | tf_op jit(solution)/shard_map/all_to_all | solution.py:49
  264.3 7.7 gather_fusion.2
  272.0 9.3 %convert_bitcast_fusion = bf16[2,64,74,192]{3,2,1,0:T(8,128)(2,1)} fusion(bf16[2,64,192,128]{3,2,1,0:T(8,128)(2,1)} %bitcast.40, pred[2,64]{1,0:T(4,128)(4,1)S(1)} %compare_and_fusion.1, bf16[2,64,74,128]{3,1,2,0:T(8,128)(2,1)S(1)} %copy-done.4), kind=kOutput, calls=%fused_computation.13 | convolution fusion | flops 470532096 | bytes 12353664 | tf_op jit(solution)/shard_map/vjcp,vjdp->vjcd/dot_general | solution.py:51
  281.3 4.3 fusion.36
  285.6 0.6 fusion.11
  286.2 0.7 add_convert_fusion
  286.9 0.3 copy.48
  287.2 0.7 reshape.194
  288.0 4.5 convolution_bitcast_fusion
  292.5 9.0 copy.57
  301.6 1.2 copy-done.6
  302.8 1.7 reshape.197
  304.5 83.7 %reduce-scatter.4.cloned.1.call-done = f32[192,2738]{1,0:T(8,128)} async-done(((f32[768,2738]{1,0:T(8,128)}), f32[192,2738]{1,0:T(8,128)}) %reduce-scatter.4.cloned.1.call-update) | async-done | bytes 2102800 | tf_op jit(solution)/shard_map/reduce_scatter | solution.py:65
  388.2 3.4 copy.58
  391.6 2.2 multiply_reduce_fusion
  393.8 11.2 %psum.14 = f32[2738]{0:T(1024)S(1)} all-reduce(f32[2738]{0:T(1024)S(1)} %multiply_reduce_fusion), channel_id=1, replica_groups=mesh['view'=64,'feat'=4] {'feat'}, use_global_device_ids=true, to_apply=%region_5.6 | all-reduce | flops 2738 | bytes 21904 | tf_op jit(solution)/shard_map/psum | solution.py:73
  405.0 1.9 multiply_reduce_fusion.1
  406.9 20.1 %psum.15 = f32[2738]{0:T(1024)S(1)} all-reduce(f32[2738]{0:T(1024)S(1)} %multiply_reduce_fusion.1), channel_id=1, replica_groups=mesh['view'=64,'feat'=4] {'feat'}, use_global_device_ids=true, to_apply=%region_7.8 | all-reduce | flops 2738 | bytes 21904 | tf_op jit(solution)/shard_map/psum | solution.py:78
  427.0 3.0 divide_convert_fusion
  430.1 58.4 %all-gather.4.cloned.1.call-done = bf16[768,2738]{1,0:T(8,128)(2,1)} async-done(((bf16[192,2738]{1,0:T(8,128)(2,1)}), bf16[768,2738]{1,0:T(8,128)(2,1)}) %all-gather.4.cloned.1.call-update) | async-done | bytes 4205584 | tf_op jit(solution)/shard_map/all_gather | solution.py:82
  488.5 5.1 fusion.37
  493.6 3.2 convolution_convert_fusion
  496.8 1.2 copy.50
  498.0 0.7 reshape.195
  498.7 0.8 convolution_convert_fusion.1
  499.6 0.8 convolution_convert_fusion.2
  500.4 0.8 pad_maximum_fusion
  501.2 0.9 copy-done.5
  502.1 7.4 fusion.5
  509.5 12.5 %gather_fusion.3 = bf16[192,192,128]{2,1,0:T(8,128)(2,1)} fusion(bf16[128,192,128]{2,1,0:T(8,128)(2,1)} %bitcast.38, s32[1024]{0:T(1024)S(1)} %pad_clamp_fusion.2), kind=kCustom, calls=%fused_computation.3 | custom fusion | bytes 18875136 | tf_op jit(solution)/shard_map/jit(_take)/gather | solution.py:102
  522.0 5.9 select_select_fusion
  527.9 307.4 %all_to_all.20 = bf16[192,192,128]{2,1,0:T(8,128)(2,1)} all-to-all(bf16[192,192,128]{2,1,0:T(8,128)(2,1)S(1)} %select_select_fusion), channel_id=1, replica_groups=mesh['view'=64,'feat'=4] {'view'}, dimensions={0} | all-to-all | bytes 18874368 | tf_op jit(solution)/shard_map/all_to_all | solution.py:103
  835.4 12.2 %convert_element_type.45 = f32[192,192,128]{2,1,0:T(8,128)} convert(bf16[192,192,128]{2,1,0:T(8,128)(2,1)} %all_to_all.20) | non-fusion elementwise | flops 4718592 | bytes 28311552 | tf_op jit(solution)/shard_map/convert_element_type | solution.py:105
  847.6 3.4 broadcast_in_dim.79
  850.9 47.1 %scatter_fusion = f32[64,192,128]{2,1,0:T(8,128)} fusion(f32[64,192,128]{2,1,0:T(8,128)} %broadcast_in_dim.79, s32[192]{0:T(256)S(1)} %reshape.232, f32[192,192,128]{2,1,0:T(8,128)} %convert_element_type.45), kind=kCustom, calls=%fused_computation.4 | custom fusion | flops 4718592 | bytes 56623872 | tf_op jit(solution)/shard_map/scatter-add | solution.py:104
  898.0 5.0 convert_element_type.46
  903.1 14.5 %reduce_sum.61 = f32[192,768]{1,0:T(8,128)} reduce(f32[64,192,768]{2,1,0:T(8,128)} %bitcast.39, f32[]{:T(128)} %constant.39.clone.1), dimensions={0}, to_apply=%region_9.10 | reduce | flops 9289728 | bytes 38338564 | tf_op jit(solution)/shard_map/reduce_sum | solution.py:13
  917.6 1.9 broadcast_multiply_fusion
  (52 shorter events, 1.9 us)
Async XLA Ops:
  7.2 28.2 %copy-start = (bf16[64,192,128]{2,1,0:T(8,128)(2,1)S(1)}, bf16[64,192,128]{2,1,0:T(8,128)(2,1)}, u32[]{:S(2)}) copy-start(bf16[64,192,128]{2,1,0:T(8,128)(2,1)} %param.7) | copy-start | bytes 9437188
  53.3 6.4 copy-start.8
  53.3 6.8 copy-start.9
  53.3 211.0 %all-to-all-start.1 = ((bf16[192,192,128]{2,1,0:T(8,128)(2,1)}), bf16[192,192,128]{2,1,0:T(8,128)(2,1)}, u32[]{:S(2)}, u32[]{:S(2)}) async-start(bf16[192,192,128]{2,1,0:T(8,128)(2,1)} %broadcast_select_fusion), calls=%async_computation.1 | async-start | bytes 18874368 | tf_op jit(solution)/shard_map/all_to_all | solution.py:49
  59.3 328.9 %reduce-scatter.4.cloned.1.call-start = ((), (), s32[]{:S(2)}) async-start(), calls=%async_computation.6 | async-start | bytes 10813440 | tf_op jit(solution)/shard_map/reduce_scatter | solution.py:65
  60.1 211.9 %copy-start.4 = (bf16[2,64,74,128]{3,1,2,0:T(8,128)(2,1)S(1)}, bf16[2,64,74,128]{3,1,2,0:T(8,128)(2,1)}, u32[]{:S(2)}) copy-start(bf16[2,64,74,128]{3,1,2,0:T(8,128)(2,1)} %param.10) | copy-start | bytes 7274500
  286.9 1.0 copy-start.7
  287.9 4.5 copy-start.3
  301.5 1.2 copy-start.6
  301.6 186.9 %all-gather.4.cloned.1.call-start = ((), (), s32[]{:S(2)}) async-start(), calls=%async_computation.4 | async-start | bytes 5406720 | tf_op jit(solution)/shard_map/all_gather | solution.py:82
  388.2 16.8 %copy-start.2 = (f32[192,2738]{1,0:T(8,128)S(1)}, f32[192,2738]{1,0:T(8,128)}, u32[]{:S(2)}) copy-start(f32[192,2738]{1,0:T(8,128)} %reduce-scatter.4.cloned.1.call-done) | copy-start | bytes 6308356
  430.0 473.0 %all-gather.6.cloned.1.call-start = ((), (), s32[]{:S(2)}) async-start(), calls=%async_computation.5 | async-start | bytes 38338560 | tf_op jit(solution)/shard_map/all_gather | solution.py:12
  500.4 1.7 copy-start.5
  903.1 16.4 %copy-start.1 = (bf16[64,192,128]{2,1,0:T(8,128)(2,1)S(1)}, bf16[64,192,128]{2,1,0:T(8,128)(2,1)}, u32[]{:S(2)}) copy-start(bf16[64,192,128]{2,1,0:T(8,128)(2,1)} %param.7) | copy-start | bytes 9437188
Sparse Core Ops, SparseCore 0:
  301.7 86.4 reduce-scatter.3
  430.2 58.2 all-gather.3
  493.7 340.6 all-gather.5
